TPU v7x, 1024 devices: a whole 4x8x16 slice. The times are simulated.
1024 devices in a mesh: temporal: 256 (over y, z, core), ulysses: 4 (over x).
Axes of the slice: x: 4, y: 8, z: 16, core: 2. Of those that a mesh axis runs over, the one named last changes fastest.
Arguments:
- queries: bfloat16 [262144, 1536], P(('temporal', 'ulysses')), may hold values from -12 to 12
- keys: bfloat16 [262144, 1536], P(('temporal', 'ulysses')), may hold values from -12 to 12
- values: bfloat16 [262144, 1536], P(('temporal', 'ulysses')), may hold values from -6 to 6
- tile_list: int32 [2048, 5], P('temporal'), may hold values from 0 to 2047, as said below
- counts: int32 [2048], P('temporal'), may hold values from 1 to 5, as said below
- out_weight: bfloat16 [1536, 1536], replicated, may hold values from -0.15625 to 0.15625
Outputs:
- projected: bfloat16 [262144, 1536], P(('temporal', 'ulysses'))
Inputs may be any that keep to these rules, and one draw needn't show every extreme that they name: `tile_list`: every id in row g lies within 3 of g and in the same video as g; the first entry is g itself; the first counts[g] entries are distinct; entries past counts[g] equal g. `counts`: some tile has 5 live entries.
All inputs are finite; a program needn't handle non-finite values.
Results may differ from a plain program's by a relative error of at most 0.0056.
Values may be sent and summed in bfloat16 or wider, within the bound.
A program may use at most 64 MiB of HBM per device.

v0:
```python
import math

import jax
import jax.numpy as jnp
from jax import lax
from jax.sharding import PartitionSpec as P

HD = 128
TILE = 128
REACH = 3


def extended(cells, sides, width):
    for axis, dim in sides:
        count = lax.axis_size(axis)
        ends = count - 1
        head = lax.slice_in_dim(cells, 0, width, axis=dim)
        tail = lax.slice_in_dim(cells, cells.shape[dim] - width, cells.shape[dim], axis=dim)
        cells = jnp.concatenate(
            [
                lax.ppermute(tail, axis, [(i, (i + 1) % count) for i in range(ends)]),
                cells,
                lax.ppermute(head, axis, [((i + 1) % count, i) for i in range(ends)]),
            ],
            axis=dim,
        )
    return cells


def attend_head(query_tiles, key_tiles, value_tiles, local_ids, live):
    tiles = local_ids.shape[0]
    width = query_tiles.shape[-1]
    key_rows = key_tiles[local_ids].reshape(tiles, -1, width)
    value_rows = value_tiles[local_ids].reshape(tiles, -1, width)
    scores = jnp.einsum("tqd,tkd->tqk", query_tiles, key_rows, preferred_element_type=jnp.float32)
    scores = scores * (1.0 / math.sqrt(width))
    scores = jnp.where(live[:, None, :], scores, -jnp.inf)
    highest = jnp.max(scores, axis=-1, keepdims=True)
    weights = jnp.exp(scores - highest)
    totals = jnp.sum(weights, axis=-1, keepdims=True)
    mixed = jnp.einsum(
        "tqk,tkd->tqd", weights.astype(jnp.bfloat16), value_rows, preferred_element_type=jnp.float32
    )
    return (mixed / totals).astype(jnp.bfloat16)


def on_device(queries, keys, values, tile_list, counts, out_weight):
    query_loc, key_loc, value_loc = (
        lax.all_to_all(queries, "ulysses", split_axis=1, concat_axis=0, tiled=True),
        lax.all_to_all(keys, "ulysses", split_axis=1, concat_axis=0, tiled=True),
        lax.all_to_all(values, "ulysses", split_axis=1, concat_axis=0, tiled=True),
    )
    key_value = jnp.stack([key_loc, value_loc])
    tok_rows = query_loc.shape[0]
    tiles = tok_rows // TILE
    rim_tiles = REACH
    padded = extended(key_value, (("temporal", 1),), REACH * TILE)
    padded_tiles = padded.shape[1] // TILE
    first_tile = lax.axis_index("temporal") * tiles - rim_tiles
    local_ids = tile_list - first_tile
    slot_count = tile_list.shape[1]
    slot_of = jnp.arange(slot_count * TILE, dtype=jnp.int32) // TILE
    live = slot_of[None, :] < counts[:, None]
    heads_local = query_loc.shape[1] // HD
    outputs = []
    for head_index in range(heads_local):
        low = head_index * HD
        query_tiles = query_loc[:, low : low + HD].reshape(tiles, TILE, HD)
        key_tiles = padded[0, :, low : low + HD].reshape(padded_tiles, TILE, HD)
        value_tiles = padded[1, :, low : low + HD].reshape(padded_tiles, TILE, HD)
        mixed = attend_head(query_tiles, key_tiles, value_tiles, local_ids, live)
        outputs.append(mixed.reshape(tok_rows, HD))
    joined = jnp.concatenate(outputs, axis=1)
    attended = lax.all_to_all(joined, "ulysses", split_axis=0, concat_axis=1, tiled=True)
    return jnp.dot(attended, out_weight, preferred_element_type=jnp.float32).astype(jnp.bfloat16)


def solution(mesh):
    return jax.shard_map(
        on_device,
        mesh=mesh,
        in_specs=(
            P(("temporal", "ulysses"), None),
            P(("temporal", "ulysses"), None),
            P(("temporal", "ulysses"), None),
            P("temporal", None),
            P("temporal"),
            P(),
        ),
        out_specs=P(("temporal", "ulysses"), None),
        check_vma=False,
    )
```

profile of v0, /device:TPU:56, one launch (start us, length us, event | category | flops | bytes accessed | tf_op | source)
XLA Modules:
  0.0 123.9 jit_solution(6795692424474229700)
XLA Ops:
  0.0 0.0 copy-start.7
  0.0 2.4 %copy.39 = bf16[256,1536]{0,1:T(8,128)(2,1)} copy(bf16[256,1536]{1,0:T(8,128)(2,1)} %param.7) | data formatting | bytes 1572864 | tf_op args[1]
  2.4 0.0 copy-start.8
  2.4 4.4 %all-to-all-start = ((bf16[256,4,384]{0,2,1:T(8,128)(2,1)}), bf16[256,4,384]{0,2,1:T(8,128)(2,1)S(1)}, u32[]{:S(2)}, u32[]{:S(2)}) async-start(bf16[256,4,384]{0,2,1:T(8,128)(2,1)} %bitcast), calls=%async_computation | async-start | bytes 1572864 | tf_op jit(solution)/shard_map/all_to_all | solution.py:50
  6.8 0.0 copy-done.7
  6.8 1.2 copy.41
  7.9 0.0 copy-start.11
  7.9 11.1 %all-to-all-done = bf16[256,4,384]{0,2,1:T(8,128)(2,1)S(1)} async-done(((bf16[256,4,384]{0,2,1:T(8,128)(2,1)}), bf16[256,4,384]{0,2,1:T(8,128)(2,1)S(1)}, u32[]{:S(2)}, u32[]{:S(2)}) %all-to-all-start) | async-done | bytes 786464 | tf_op jit(solution)/shard_map/all_to_all | solution.py:50
  19.1 3.5 %all-to-all-start.1 = ((bf16[256,4,384]{0,2,1:T(8,128)(2,1)}), bf16[256,4,384]{0,2,1:T(8,128)(2,1)S(1)}, u32[]{:S(2)}, u32[]{:S(2)}) async-start(bf16[256,4,384]{0,2,1:T(8,128)(2,1)} %bitcast.3), calls=%async_computation.1 | async-start | bytes 1572864 | tf_op jit(solution)/shard_map/all_to_all | solution.py:51
  22.6 0.0 copy-done.8
  22.6 0.3 copy.43
  22.9 1.2 copy.44
  24.0 0.0 copy-done.11
  24.0 0.4 copy.40
  24.4 0.0 copy-start.12
  24.4 9.6 %all-to-all-done.1 = bf16[256,4,384]{0,2,1:T(8,128)(2,1)S(1)} async-done(((bf16[256,4,384]{0,2,1:T(8,128)(2,1)}), bf16[256,4,384]{0,2,1:T(8,128)(2,1)S(1)}, u32[]{:S(2)}, u32[]{:S(2)}) %all-to-all-start.1) | async-done | bytes 786464 | tf_op jit(solution)/shard_map/all_to_all | solution.py:51
  34.0 3.5 %all-to-all-start.2 = ((bf16[256,4,384]{2,0,1:T(8,128)(2,1)}), bf16[256,4,384]{2,0,1:T(8,128)(2,1)S(1)}, u32[]{:S(2)}, u32[]{:S(2)}) async-start(bf16[256,4,384]{2,0,1:T(8,128)(2,1)} %copy.44), calls=%async_computation.2 | async-start | bytes 1572864 | tf_op jit(solution)/shard_map/all_to_all | solution.py:49
  37.5 0.4 copy.42
  37.8 1.2 pad_maximum_fusion.3
  39.0 1.9 %collective-permute-start = (bf16[2,384,384]{2,1,0:T(8,128)(2,1)}, bf16[2,384,384]{2,1,0:T(8,128)(2,1)S(1)}, u32[]{:S(2)}, u32[]{:S(2)}) collective-permute-start(bf16[2,384,384]{2,1,0:T(8,128)(2,1)} %get-tuple-element.16), channel_id=1, source_target_pairs={{0,4},{4,8},{8,12},{12,16},{16,20},{20,24},{24,28},{28,32},{32,36}... | collective-permute-start | bytes 1769480 | tf_op jit(solution)/shard_map/ppermute | solution.py:21
  40.9 16.2 %collective-permute-start.1 = (bf16[2,384,384]{2,1,0:T(8,128)(2,1)}, bf16[2,384,384]{2,1,0:T(8,128)(2,1)}, u32[]{:S(2)}, u32[]{:S(2)}) collective-permute-start(bf16[2,384,384]{2,1,0:T(8,128)(2,1)} %get-tuple-element.17), channel_id=1, source_target_pairs={{4,0},{8,4},{12,8},{16,12},{20,16},{24,20},{28,24},{32,28},{36,32}... | collective-permute-start | bytes 1769480 | tf_op jit(solution)/shard_map/ppermute | solution.py:23
  57.1 0.1 reshape.103
  57.2 0.0 copy-done.12
  57.2 0.1 broadcast_compare_fusion
  57.3 0.0 all-to-all-done.2
  57.3 1.0 fusion.55
  58.2 4.7 %collective-permute-done = bf16[2,384,384]{2,1,0:T(8,128)(2,1)S(1)} collective-permute-done((bf16[2,384,384]{2,1,0:T(8,128)(2,1)}, bf16[2,384,384]{2,1,0:T(8,128)(2,1)S(1)}, u32[]{:S(2)}, u32[]{:S(2)}) %collective-permute-start) | collective-permute-done | bytes 589856 | tf_op jit(solution)/shard_map/ppermute | solution.py:21
  62.9 1.9 %collective-permute-done.1 = bf16[2,384,384]{2,1,0:T(8,128)(2,1)} collective-permute-done((bf16[2,384,384]{2,1,0:T(8,128)(2,1)}, bf16[2,384,384]{2,1,0:T(8,128)(2,1)}, u32[]{:S(2)}, u32[]{:S(2)}) %collective-permute-start.1) | collective-permute-done | bytes 589856 | tf_op jit(solution)/shard_map/ppermute | solution.py:23
  64.8 2.8 %pad_maximum_fusion = bf16[2,1792,384]{2,1,0:T(8,128)(2,1)S(1)} fusion(bf16[2,384,384]{2,1,0:T(8,128)(2,1)} %collective-permute-done.1, bf16[1,1024,384]{2,1,0:T(8,128)(2,1)S(1)} %bitcast.87, bf16[1,1024,384]{2,1,0:T(8,128)(2,1)S(1)} %bitcast.85, bf16[2,384,384]{2,1,0:T(8,128)(2,1)S(1)} %collective-permute-done), kind=kLoop, calls=%fused_computation.6 | loop fusion | flops 11010048 | bytes 5505024 | tf_op jit(solution)/shard_map/concatenate | solution.py:19
  67.6 0.5 fusion.54
  68.1 1.9 %gather_fusion = bf16[40,128,128]{2,1,0:T(8,128)(2,1)} fusion(bf16[14,128,128]{2,1,0:T(8,128)(2,1)S(1)} %bitcast.93, s32[1024]{0:T(1024)S(1)} %pad_clamp_fusion), kind=kCustom, calls=%fused_computation | custom fusion | bytes 2621600 | tf_op jit(solution)/shard_map/gather | solution.py:33
  70.0 1.8 %gather_fusion.4 = bf16[40,128,128]{2,1,0:T(8,128)(2,1)} fusion(bf16[14,128,128]{2,1,0:T(8,128)(2,1)S(1)} %bitcast.92, s32[1024]{0:T(1024)S(1)} %pad_clamp_fusion), kind=kCustom, calls=%fused_computation.4 | custom fusion | bytes 2621600 | tf_op jit(solution)/shard_map/gather | solution.py:33
  71.8 1.8 %gather_fusion.2 = bf16[40,128,128]{2,1,0:T(8,128)(2,1)} fusion(bf16[14,128,128]{2,1,0:T(8,128)(2,1)S(1)} %bitcast.91, s32[1024]{0:T(1024)S(1)} %pad_clamp_fusion), kind=kCustom, calls=%fused_computation.2 | custom fusion | bytes 2621600 | tf_op jit(solution)/shard_map/gather | solution.py:33
  73.6 1.9 %gather_fusion.1 = bf16[40,128,128]{2,1,0:T(8,128)(2,1)} fusion(bf16[14,128,128]{2,1,0:T(8,128)(2,1)S(1)} %bitcast.90, s32[1024]{0:T(1024)S(1)} %pad_clamp_fusion), kind=kCustom, calls=%fused_computation.1 | custom fusion | bytes 2621600 | tf_op jit(solution)/shard_map/gather | solution.py:34
  75.5 0.0 copy-start
  75.5 0.0 copy-start.5
  75.5 2.0 %fusion.56 = f32[8,640,128]{2,1,0:T(8,128)S(1)} fusion(bf16[8,640,128]{2,1,0:T(8,128)(2,1)} %bitcast.95, bf16[8,128,128]{2,1,0:T(8,128)(2,1)} %bitcast.105), kind=kOutput, calls=%fused_computation.68 | convolution fusion | flops 167772160 | bytes 4194304 | tf_op jit(solution)/shard_map/tqd,tkd->tqk/dot_general | solution.py:35
  77.5 0.0 copy-start.2
  77.5 0.0 copy-start.9
  77.5 0.0 copy-done
  77.5 0.0 copy-done.5
  77.5 2.1 %bitcast_reduce_fusion.2 = (f32[8,128]{1,0:T(8,128)S(1)}, f32[8,640,128]{2,1,0:T(8,128)S(1)}) fusion(pred[8,640]{1,0:T(8,128)(4,1)S(1)} %broadcast_compare_fusion, bf16[8,640,128]{2,1,0:T(8,128)(2,1)S(1)} %bitcast.94, bf16[8,128,128]{2,1,0:T(8,128)(2,1)S(1)} %bitcast.104), kind=kOutput, calls=%fused_computation.14 | convolution fusion | flops 169737216 | bytes 4203520 | tf_op jit(solution)/shard_map/tqd,tkd->tqk/dot_general | solution.py:35
  79.6 0.0 copy-done.2
  79.6 0.0 copy-done.9
  79.6 0.0 copy-start.3
  79.6 4.2 %fusion.3 = (f32[8,128]{1,0:T(8,128)S(1)}, f32[8,128]{1,0:T(8,128)}, f32[8,128]{1,0:T(8,128)S(1)}, f32[8,640,128]{2,1,0:T(8,128)}) fusion(f32[8,640,128]{2,1,0:T(8,128)S(1)} %get-tuple-element.22, f32[8,128]{1,0:T(8,128)S(1)} %get-tuple-element.21, pred[8,640]{1,0:T(8,128)(4,1)S(1)} %broadcast_compare_fusion, f32[8,640,128]{2,1,0:T(8,128)S(1)} %fusion.56, ...), kind=kOutput, calls=%fused_computation.20 | convolution fusion | flops 174322688 | bytes 9458688 | tf_op jit(solution)/shard_map/tqd,tkd->tqk/dot_general | solution.py:35
  83.9 0.0 copy-done.3
  83.9 3.3 %fusion.30 = bf16[8,128,128]{2,1,0:T(8,128)(2,1)} fusion(bf16[8,640,128]{2,1,0:T(8,128)(2,1)S(1)} %bitcast.101, f32[8,640,128]{2,1,0:T(8,128)S(1)} %get-tuple-element.22, f32[8,128]{1,0:T(8,128)S(1)} %get-tuple-element.21, pred[8,640]{1,0:T(8,128)(4,1)S(1)} %broadcast_compare_fusion, f32[8,128]{1,0:T(8,128)S(1)} %get-tuple-element.5), kind=kOutput, calls=%fused_computation.42 | convolution fusion | flops 170655744 | bytes 4207616 | tf_op jit(solution)/shard_map/tqk,tkd->tqd/dot_general | solution.py:41
  87.1 1.8 %copy.48 = bf16[4,256,128]{1,2,0:T(8,128)(2,1)} copy(bf16[4,256,128]{2,1,0:T(8,128)(2,1)} %bitcast.108) | data formatting | bytes 524288 | tf_op jit(solution)/shard_map/concatenate | solution.py:73
  88.9 1.9 %gather_fusion.3 = bf16[40,128,128]{2,1,0:T(8,128)(2,1)} fusion(bf16[14,128,128]{2,1,0:T(8,128)(2,1)S(1)} %bitcast.89, s32[1024]{0:T(1024)S(1)} %pad_clamp_fusion), kind=kCustom, calls=%fused_computation.3 | custom fusion | bytes 2621600 | tf_op jit(solution)/shard_map/gather | solution.py:34
  90.8 0.0 copy-start.1
  90.8 3.5 %fusion.5 = (f32[8,128]{1,0:T(8,128)S(1)}, f32[8,128]{1,0:T(8,128)S(1)}) fusion(f32[8,640,128]{2,1,0:T(8,128)} %get-tuple-element.23, f32[8,128]{1,0:T(8,128)} %get-tuple-element.6, pred[8,640]{1,0:T(8,128)(4,1)S(1)} %broadcast_compare_fusion, f32[8,128]{1,0:T(8,128)S(1)} %get-tuple-element.7, f32[8,640,128]{2,1,0:T(8,128)S(1)} %fusion.56), kind=kLoop, calls=%fused_computation.22 | loop fusion | flops 5240832 | bytes 5264384 | tf_op jit(solution)/shard_map/reduce_sum | solution.py:40
  94.3 0.0 copy-done.1
  94.3 0.0 copy-done.4
  94.3 0.0 copy-done.10
  94.3 3.3 %fusion.36 = bf16[8,128,128]{2,1,0:T(8,128)(2,1)} fusion(bf16[8,640,128]{2,1,0:T(8,128)(2,1)S(1)} %bitcast.102, f32[8,640,128]{2,1,0:T(8,128)S(1)} %copy-done.1, f32[8,128]{1,0:T(8,128)S(1)} %copy-done.10, pred[8,640]{1,0:T(8,128)(4,1)S(1)} %broadcast_compare_fusion, f32[8,128]{1,0:T(8,128)S(1)} %get-tuple-element.8), kind=kOutput, calls=%fused_computation.44 | convolution fusion | flops 170655744 | bytes 4207616 | tf_op jit(solution)/shard_map/tqk,tkd->tqd/dot_general | solution.py:41
  97.6 1.1 copy.49
  98.7 1.9 %gather_fusion.5 = bf16[40,128,128]{2,1,0:T(8,128)(2,1)} fusion(bf16[14,128,128]{2,1,0:T(8,128)(2,1)S(1)} %bitcast.88, s32[1024]{0:T(1024)S(1)} %pad_clamp_fusion), kind=kCustom, calls=%fused_computation.5 | custom fusion | bytes 2621600 | tf_op jit(solution)/shard_map/gather | solution.py:34
  100.6 3.8 %fusion.42 = bf16[8,128,128]{2,1,0:T(8,128)(2,1)} fusion(bf16[8,640,128]{2,1,0:T(8,128)(2,1)} %bitcast.103, f32[8,640,128]{2,1,0:T(8,128)S(1)} %fusion.56, f32[8,128]{1,0:T(8,128)S(1)} %get-tuple-element.7, pred[8,640]{1,0:T(8,128)(4,1)S(1)} %broadcast_compare_fusion, f32[8,128]{1,0:T(8,128)S(1)} %get-tuple-element.9), kind=kOutput, calls=%fused_computation.46 | convolution fusion | flops 170655744 | bytes 4207616 | tf_op jit(solution)/shard_map/tqk,tkd->tqd/dot_general | solution.py:41
  104.4 1.1 copy.50
  105.5 0.0 copy-done.6
  105.5 0.1 pad_maximum_fusion.1
  105.5 13.8 %all_to_all.67 = bf16[4,256,384]{1,2,0:T(8,128)(2,1)S(1)} all-to-all(bf16[4,256,384]{1,2,0:T(8,128)(2,1)S(1)} %pad_maximum_fusion.1), channel_id=1, replica_groups=mesh['temporal'=256,'ulysses'=4] {'ulysses'}, dimensions={0} | all-to-all | bytes 1572864 | tf_op jit(solution)/shard_map/all_to_all | solution.py:74
  119.3 4.6 %convolution_convert_fusion = bf16[256,1536]{1,0:T(8,128)(2,1)} fusion(bf16[256,1536]{0,1:T(8,128)(2,1)S(1)} %bitcast.106, bf16[1536,1536]{1,0:T(8,128)(2,1)} %param.11), kind=kOutput, calls=%fused_computation.19 | convolution fusion | flops 1208352768 | bytes 6291456 | tf_op jit(solution)/shard_map/dot_general | solution.py:75
  (6 shorter events, 0.0 us)
Async XLA Ops:
  0.0 6.8 %copy-start.7 = (bf16[256,1536]{1,0:T(8,128)(2,1)S(1)}, bf16[256,1536]{1,0:T(8,128)(2,1)}, u32[]{:S(2)}) copy-start(bf16[256,1536]{1,0:T(8,128)(2,1)} %param.8) | copy-start | bytes 2359300
  2.4 20.2 %copy-start.8 = (bf16[256,1536]{1,0:T(8,128)(2,1)S(1)}, bf16[256,1536]{1,0:T(8,128)(2,1)}, u32[]{:S(2)}) copy-start(bf16[256,1536]{1,0:T(8,128)(2,1)} %param.6) | copy-start | bytes 2359300
  2.4 16.7 %all-to-all-start = ((bf16[256,4,384]{0,2,1:T(8,128)(2,1)}), bf16[256,4,384]{0,2,1:T(8,128)(2,1)S(1)}, u32[]{:S(2)}, u32[]{:S(2)}) async-start(bf16[256,4,384]{0,2,1:T(8,128)(2,1)} %bitcast), calls=%async_computation | async-start | bytes 1572864 | tf_op jit(solution)/shard_map/all_to_all | solution.py:50
  7.9 16.1 %copy-start.11 = (s32[8,5]{1,0:T(8,128)S(1)}, s32[8,5]{1,0:T(8,128)}, u32[]{:S(2)}) copy-start(s32[8,5]{1,0:T(8,128)} %param.9) | copy-start | bytes 484
  19.1 14.9 %all-to-all-start.1 = ((bf16[256,4,384]{0,2,1:T(8,128)(2,1)}), bf16[256,4,384]{0,2,1:T(8,128)(2,1)S(1)}, u32[]{:S(2)}, u32[]{:S(2)}) async-start(bf16[256,4,384]{0,2,1:T(8,128)(2,1)} %bitcast.3), calls=%async_computation.1 | async-start | bytes 1572864 | tf_op jit(solution)/shard_map/all_to_all | solution.py:51
  24.4 32.8 %copy-start.12 = (s32[8]{0:T(128)S(1)}, s32[8]{0:T(128)}, u32[]{:S(2)}) copy-start(s32[8]{0:T(128)} %param.10) | copy-start | bytes 100
  34.0 23.3 %all-to-all-start.2 = ((bf16[256,4,384]{2,0,1:T(8,128)(2,1)}), bf16[256,4,384]{2,0,1:T(8,128)(2,1)S(1)}, u32[]{:S(2)}, u32[]{:S(2)}) async-start(bf16[256,4,384]{2,0,1:T(8,128)(2,1)} %copy.44), calls=%async_computation.2 | async-start | bytes 1572864 | tf_op jit(solution)/shard_map/all_to_all | solution.py:49
  39.0 23.9 %collective-permute-start = (bf16[2,384,384]{2,1,0:T(8,128)(2,1)}, bf16[2,384,384]{2,1,0:T(8,128)(2,1)S(1)}, u32[]{:S(2)}, u32[]{:S(2)}) collective-permute-start(bf16[2,384,384]{2,1,0:T(8,128)(2,1)} %get-tuple-element.16), channel_id=1, source_target_pairs={{0,4},{4,8},{8,12},{12,16},{16,20},{20,24},{24,28},{28,32},{32,36}... | collective-permute-start | bytes 1769480 | tf_op jit(solution)/shard_map/ppermute | solution.py:21
  40.9 23.9 %collective-permute-start.1 = (bf16[2,384,384]{2,1,0:T(8,128)(2,1)}, bf16[2,384,384]{2,1,0:T(8,128)(2,1)}, u32[]{:S(2)}, u32[]{:S(2)}) collective-permute-start(bf16[2,384,384]{2,1,0:T(8,128)(2,1)} %get-tuple-element.17), channel_id=1, source_target_pairs={{4,0},{8,4},{12,8},{16,12},{20,16},{24,20},{28,24},{32,28},{36,32}... | collective-permute-start | bytes 1769480 | tf_op jit(solution)/shard_map/ppermute | solution.py:23
  75.5 2.0 %copy-start = (bf16[40,128,128]{2,1,0:T(8,128)(2,1)S(1)}, bf16[40,128,128]{2,1,0:T(8,128)(2,1)}, u32[]{:S(2)}) copy-start(bf16[40,128,128]{2,1,0:T(8,128)(2,1)} %gather_fusion) | copy-start | bytes 3932164
  75.5 2.0 %copy-start.5 = (bf16[1024,128]{1,0:T(8,128)(2,1)S(1)}, bf16[1024,128]{1,0:T(8,128)(2,1)}, u32[]{:S(2)}) copy-start(bf16[1024,128]{1,0:T(8,128)(2,1)} %get-tuple-element.20) | copy-start | bytes 786436
  77.5 2.2 %copy-start.2 = (bf16[40,128,128]{2,1,0:T(8,128)(2,1)S(1)}, bf16[40,128,128]{2,1,0:T(8,128)(2,1)}, u32[]{:S(2)}) copy-start(bf16[40,128,128]{2,1,0:T(8,128)(2,1)} %gather_fusion.2) | copy-start | bytes 3932164
  77.5 2.2 %copy-start.9 = (bf16[1024,128]{1,0:T(8,128)(2,1)S(1)}, bf16[1024,128]{1,0:T(8,128)(2,1)}, u32[]{:S(2)}) copy-start(bf16[1024,128]{1,0:T(8,128)(2,1)} %get-tuple-element.18) | copy-start | bytes 786436
  79.6 4.2 %copy-start.3 = (bf16[40,128,128]{2,1,0:T(8,128)(2,1)S(1)}, bf16[40,128,128]{2,1,0:T(8,128)(2,1)}, u32[]{:S(2)}) copy-start(bf16[40,128,128]{2,1,0:T(8,128)(2,1)} %gather_fusion.1) | copy-start | bytes 3932164
  90.8 3.5 %copy-start.1 = (f32[8,640,128]{2,1,0:T(8,128)S(1)}, f32[8,640,128]{2,1,0:T(8,128)}, u32[]{:S(2)}) copy-start(f32[8,640,128]{2,1,0:T(8,128)} %get-tuple-element.23) | copy-start | bytes 7864324
  90.8 3.5 %copy-start.4 = (bf16[40,128,128]{2,1,0:T(8,128)(2,1)S(1)}, bf16[40,128,128]{2,1,0:T(8,128)(2,1)}, u32[]{:S(2)}) copy-start(bf16[40,128,128]{2,1,0:T(8,128)(2,1)} %gather_fusion.3) | copy-start | bytes 3932164
  90.8 3.5 %copy-start.10 = (f32[8,128]{1,0:T(8,128)S(1)}, f32[8,128]{1,0:T(8,128)}, u32[]{:S(2)}) copy-start(f32[8,128]{1,0:T(8,128)} %get-tuple-element.6) | copy-start | bytes 12292
  100.6 4.9 %copy-start.6 = (bf16[4,256,128]{1,2,0:T(8,128)(2,1)S(1)}, bf16[4,256,128]{1,2,0:T(8,128)(2,1)}, u32[]{:S(2)}) copy-start(bf16[4,256,128]{1,2,0:T(8,128)(2,1)} %copy.48) | copy-start | bytes 786436
where the time goes:
time: 124 us
  starting transfers between devices  29.5 us (24%)
  waiting for transfers between devices  27.2 us (22%)
  matrix products  23.3 us (19%)
  local copies, waits for them, and re-layouts  22.3 us (18%)
  blocking collectives  13.8 us (11%)
  other arithmetic  7.61 us (6%)
    ppermute x1, starting transfers between devices, extended(): lax.ppermute(head, axis, [((i + 1) % count, i) for i in range(ends)])  16.2 us
    all_to_all x1, blocking collectives, on_device(): lax.all_to_all(joined, 'ulysses', split_axis=0, concat_axis=1, tiled=True)  13.8 us
    all_to_all x1, waiting for transfers between devices, on_device(): lax.all_to_all(keys, 'ulysses', split_axis=1, concat_axis=0, tiled=True)  11.1 us
    dot_general x3, matrix products, attend_head(): jnp.einsum('tqk,tkd->tqd', weights.astype(jnp.bfloat16), value_rows, pref...  10.4 us
    all_to_all x1, waiting for transfers between devices, on_device(): lax.all_to_all(values, 'ulysses', split_axis=1, concat_axis=0, tiled=True)  9.57 us
    dot_general x3, matrix products, attend_head(): jnp.einsum('tqd,tkd->tqk', query_tiles, key_rows, preferred_element_type=...  8.29 us
    gather x3, local copies, waits for them, and re-layouts, attend_head(): value_rows = value_tiles[local_ids].reshape(tiles, -1, width)  5.58 us
    gather x3, local copies, waits for them, and re-layouts, attend_head(): key_rows = key_tiles[local_ids].reshape(tiles, -1, width)  5.55 us
  transfers between devices with their start and end apart: 5, of which 4 were waited for; matrix products, arithmetic and copies ran while one was open for 4% of the time, Pallas kernels for 0%

commit v1 on v0

v1 whole, which is shorter than its diff:
```python
import functools
import math

import jax
import jax.numpy as jnp
from jax import lax
from jax.experimental import pallas as pl
from jax.experimental.pallas import tpu as pltpu
from jax.sharding import PartitionSpec as P

HD = 128
TILE = 128
REACH = 3
RING = 4
PAIR = 2
LOCAL_HEADS = 3
OWN = RING * PAIR
SPAN = OWN + 2 * REACH
SLOTS = 5
MESH = pl.DeviceIdType.MESH
NEG = -1e30
COLS = 256


def kernel(groups, tl_ref, cnt_ref, q_ref, k_ref, v_ref, w_ref, out_ref,
           kb0, kb1, kb2, vb0, vb1, vb2, qb0, qb1, qb2, ab0, ab1, ab2, ob0, ob1, ob2,
           wb0, wb1, wb2, to_right, to_left, acc, done,
           ssem, rsem, hssem, hrsem, lsem, wsem, osem):
    t = lax.axis_index("temporal")
    u = lax.axis_index("ulysses")
    right, left, far = lax.rem(u + 1, RING), lax.rem(u + 3, RING), lax.rem(u + 2, RING)
    after, before = lax.rem(t + 1, groups), lax.rem(t + groups - 1, groups)
    bufs = ((kb0, kb1, kb2), (vb0, vb1, vb2), (qb0, qb1, qb2))
    sources = (k_ref, v_ref, q_ref)
    joined, sent, weights = (ab0, ab1, ab2), (ob0, ob1, ob2), (wb0, wb1, wb2)

    def remote(src, dst, kind, index, device):
        return functools.partial(
            pltpu.make_async_remote_copy,
            src_ref=src, dst_ref=dst, send_sem=ssem.at[index, kind], recv_sem=rsem.at[index, kind],
            device_id=device, device_id_type=MESH)

    def columns(x, head):
        return pl.ds(pl.multiple_of((x * LOCAL_HEADS + head) * HD, HD), HD)

    def place(x):
        return pl.ds(pl.multiple_of(x * HD, HD), HD)

    def stage(s):
        head, kind = divmod(s, 3)
        base = REACH if kind < 2 else 0
        return sources[kind], bufs[kind][head], base, head

    def local_copy(s):
        src, buf, base, head = stage(s)
        return pltpu.make_async_copy(
            src.at[:, :, columns(u, head)], buf.at[pl.ds(base + PAIR * u, PAIR)], lsem.at[s])

    def weight_copy(head):
        return pltpu.make_async_copy(w_ref.at[:, head], weights[head], wsem.at[head])

    def first_hops(s, x):
        src, buf, base, head = stage(s)
        return (
            remote(src.at[0, :, columns(far, head)], to_right.at[s], 0, s, (t, right)),
            remote(src.at[1, :, columns(far, head)], to_left.at[s], 1, s, (t, left)),
            remote(src.at[:, :, columns(right, head)], buf.at[pl.ds(base + PAIR * x[0], PAIR)], 2, s, (t, right)),
            remote(src.at[:, :, columns(left, head)], buf.at[pl.ds(base + PAIR * x[1], PAIR)], 3, s, (t, left)),
        )

    def second_hops(s, x):
        src, buf, base, head = stage(s)
        return (
            remote(to_right.at[s], buf.at[base + PAIR * x[0]], 4, s, (t, right)),
            remote(to_left.at[s], buf.at[base + PAIR * x[1] + 1], 5, s, (t, left)),
        )

    def start(s):
        for copy in first_hops(s, (u, u)):
            copy().start()

    def relay(s):
        arrive = first_hops(s, (left, right))
        onward = second_hops(s, (left, right))
        for side in range(2):
            arrive[side]().wait_recv()
            onward[side]().start()

    def collect(s):
        arrive = first_hops(s, (left, right))
        arrive[2]().wait_recv()
        arrive[3]().wait_recv()
        for copy in second_hops(s, (far, far)):
            copy().wait_recv()
        local_copy(s).wait()

    def halo(head, kind):
        buf = bufs[kind][head]
        return tuple(
            functools.partial(
                pltpu.make_async_remote_copy,
                src_ref=buf.at[pl.ds(low, REACH)], dst_ref=buf.at[pl.ds(high, REACH)],
                send_sem=hssem.at[head, kind, side], recv_sem=hrsem.at[head, kind, side],
                device_id=(there, u), device_id_type=MESH)
            for side, (low, high, there) in enumerate(((OWN, 0, after), (REACH, REACH + OWN, before))))

    def halo_start(head, kind):
        for copy in halo(head, kind):
            copy().start()

    def halo_wait(head):
        for kind in range(2):
            for copy in halo(head, kind):
                copy().wait_recv()

    def out_first(head, x):
        s = 9 + head
        buf, dst = sent[head], joined[head]
        return (
            remote(buf.at[1, 0], to_right.at[s], 0, s, (t, right)),
            remote(buf.at[1, 1], to_left.at[s], 1, s, (t, left)),
            remote(buf.at[0], dst.at[:, :, place(x[0])], 2, s, (t, right)),
            remote(buf.at[2], dst.at[:, :, place(x[1])], 3, s, (t, left)),
        )

    def out_second(head, x):
        s = 9 + head
        dst = joined[head]
        return (
            remote(to_right.at[s], dst.at[0, :, place(x[0])], 4, s, (t, right)),
            remote(to_left.at[s], dst.at[1, :, place(x[1])], 5, s, (t, left)),
        )

    def out_start(head, parts):
        copies = out_first(head, (u, u))
        for part in parts:
            copies[part]().start()

    def out_relay(head):
        arrive = out_first(head, (left, right))
        onward = out_second(head, (left, right))
        for side in range(2):
            arrive[side]().wait_recv()
            onward[side]().start()

    def out_collect(head):
        arrive = out_first(head, (left, right))
        arrive[2]().wait_recv()
        arrive[3]().wait_recv()
        for copy in out_second(head, (far, far)):
            copy().wait_recv()

    first_tile = t * OWN - REACH
    rate = math.log2(math.e) / math.sqrt(HD)

    def attend(head, offset):
        kb, vb, qb = bufs[0][head], bufs[1][head], bufs[2][head]
        base = PAIR * lax.rem(u + offset, RING)
        row = lax.broadcasted_iota(jnp.int32, (1, SLOTS * TILE), 1)
        for i in range(PAIR):
            g = base + i
            ids = [jnp.clip(tl_ref[g, slot] - first_tile, 0, SPAN - 1) for slot in range(SLOTS)]
            key_rows = jnp.concatenate([kb[n] for n in ids], axis=0)
            scores = lax.dot_general(qb[g], key_rows, (((1,), (1,)), ((), ())),
                                     preferred_element_type=jnp.float32)
            scores = jnp.where(row < cnt_ref[g] * TILE, scores, NEG)
            top = jnp.max(scores, axis=-1, keepdims=True)
            parts = jnp.exp2((scores - top) * rate)
            totals = jnp.sum(parts, axis=-1, keepdims=True)
            value_rows = jnp.concatenate([vb[n] for n in ids], axis=0)
            mixed = jnp.dot(parts.astype(jnp.bfloat16), value_rows, preferred_element_type=jnp.float32)
            mixed = (mixed / totals).astype(jnp.bfloat16)
            if offset == 0:
                joined[head][i, :, place(u)] = mixed
            else:
                sent[head][offset - 1, i] = mixed

    def project(head):
        rows = joined[head][...].reshape(PAIR * TILE, RING * HD)

        def block(c, carry):
            cols = pl.ds(pl.multiple_of(c * COLS, COLS), COLS)
            w = weights[head][:, :, cols].reshape(RING * HD, COLS)
            part = jnp.dot(rows, w, preferred_element_type=jnp.float32)
            if head > 0:
                part = part + acc[:, cols]
            if head < LOCAL_HEADS - 1:
                acc[:, cols] = part
            else:
                done[:, cols] = part.astype(jnp.bfloat16)
            return carry

        lax.fori_loop(0, acc.shape[1] // COLS, block, 0)

    barrier = pltpu.get_barrier_semaphore()
    for device in ((t, right), (t, left), (after, u), (before, u)):
        pl.semaphore_signal(barrier, inc=1, device_id=device, device_id_type=MESH)
    for s in range(9):
        local_copy(s).start()
    for head in range(LOCAL_HEADS):
        weight_copy(head).start()
    pl.semaphore_wait(barrier, 4)

    start(0)
    start(1)
    relay(0)
    start(2)
    relay(1)
    start(3)
    collect(0)
    halo_start(0, 0)
    relay(2)
    start(4)
    collect(1)
    halo_start(0, 1)
    relay(3)
    start(5)
    collect(2)
    halo_wait(0)
    attend(0, 2)
    attend(0, 1)
    relay(4)
    start(6)
    collect(3)
    halo_start(1, 0)
    attend(0, 3)
    attend(0, 0)
    relay(5)
    start(7)
    out_start(0, (0, 1, 2, 3))
    collect(4)
    halo_start(1, 1)
    relay(6)
    start(8)
    out_relay(0)
    collect(5)
    halo_wait(1)
    attend(1, 2)
    attend(1, 1)
    relay(7)
    collect(6)
    halo_start(2, 0)
    attend(1, 3)
    attend(1, 0)
    relay(8)
    out_start(1, (0, 1, 2, 3))
    collect(7)
    halo_start(2, 1)
    weight_copy(0).wait()
    out_collect(0)
    project(0)
    collect(8)
    halo_wait(2)
    attend(2, 2)
    out_start(2, (0, 1))
    out_relay(1)
    attend(2, 1)
    out_start(2, (2,))
    attend(2, 3)
    out_start(2, (3,))
    out_relay(2)
    attend(2, 0)
    weight_copy(1).wait()
    out_collect(1)
    project(1)
    weight_copy(2).wait()
    out_collect(2)
    project(2)
    result = pltpu.make_async_copy(done, out_ref, osem)
    result.start()

    for s in range(9):
        for copy in first_hops(s, (u, u)) + second_hops(s, (left, right)):
            copy().wait_send()
    for head in range(LOCAL_HEADS):
        for copy in out_first(head, (u, u)) + out_second(head, (left, right)):
            copy().wait_send()
        for kind in range(2):
            for copy in halo(head, kind):
                copy().wait_send()
    result.wait()


def solution(mesh):
    groups = mesh.shape["temporal"]

    def on_device(queries, keys, values, tile_list, counts, out_weight):
        width = queries.shape[1]
        split = lambda a: a.reshape(PAIR, TILE, width)
        any_space = pl.BlockSpec(memory_space=pl.ANY)
        smem = pl.BlockSpec(memory_space=pltpu.SMEM)
        bf = jnp.bfloat16
        heads = range(LOCAL_HEADS)
        return pl.pallas_call(
            functools.partial(kernel, groups),
            out_shape=jax.ShapeDtypeStruct(queries.shape, bf),
            in_specs=[smem, smem, any_space, any_space, any_space, any_space],
            out_specs=any_space,
            scratch_shapes=(
                [pltpu.VMEM((SPAN, TILE, HD), bf) for _ in range(2) for _ in heads]
                + [pltpu.VMEM((OWN, TILE, HD), bf) for _ in heads]
                + [pltpu.VMEM((PAIR, TILE, RING * HD), bf) for _ in heads]
                + [pltpu.VMEM((RING - 1, PAIR, TILE, HD), bf) for _ in heads]
                + [pltpu.VMEM((RING, HD, width), bf) for _ in heads]
                + [pltpu.VMEM((12, TILE, HD), bf) for _ in range(2)]
                + [
                    pltpu.VMEM((PAIR * TILE, width), jnp.float32),
                    pltpu.VMEM((PAIR * TILE, width), bf),
                    pltpu.SemaphoreType.DMA((12, 6)),
                    pltpu.SemaphoreType.DMA((12, 6)),
                    pltpu.SemaphoreType.DMA((3, 2, 2)),
                    pltpu.SemaphoreType.DMA((3, 2, 2)),
                    pltpu.SemaphoreType.DMA((9,)),
                    pltpu.SemaphoreType.DMA((3,)),
                    pltpu.SemaphoreType.DMA,
                ]
            ),
            compiler_params=pltpu.CompilerParams(
                collective_id=0, has_side_effects=True, vmem_limit_bytes=56 * 1024 * 1024
            ),
        )(tile_list, counts, split(queries), split(keys), split(values),
          out_weight.reshape(RING, LOCAL_HEADS, HD, width))

    rows = P(("temporal", "ulysses"), None)
    return jax.shard_map(
        on_device,
        mesh=mesh,
        in_specs=(rows, rows, rows, P("temporal", None), P("temporal"), P()),
        out_specs=rows,
        check_vma=False,
    )
```

time: 124 us -> 68.2 us (0.55)
  the two profiles are of different devices: /device:TPU:56 before, /device:TPU:6 now
where the time goes in v1:
time: 68.2 us; the launch traced here: 67.2 us
  Pallas kernels  65.1 us (95%)
  local copies, waits for them, and re-layouts  2.06 us (3%)
    pallas_call x1, Pallas kernels, on_device(): pl.pallas_call(functools.partial(kernel, groups), out_shape=jax.ShapeDtyp...  65.1 us
    unnamed x1, local copies, waits for them, and re-layouts  2.06 us

profile of v1, /device:TPU:6, one launch (start us, length us, event | category | flops | bytes accessed | tf_op | source)
XLA Modules:
  0.0 67.2 jit_solution(32127973781878683)
XLA Ops:
  0.0 65.1 %shard_map.64 = bf16[256,1536]{1,0:T(8,128)(2,1)} custom-call(s32[8,5]{1,0:T(8,128)} %tl_ref.1, s32[8]{0:T(128)} %cnt_ref.1, bf16[2,128,1536]{2,1,0:T(8,128)(2,1)} %bitcast.5, bf16[2,128,1536]{2,1,0:T(8,128)(2,1)} %bitcast.6, bf16[2,128,1536]{2,1,0:T(8,128)(2,1)} %bitcast.7, bf16[4,3,128,1536]{3,2,1,0:T(8,128)(2,1)} %bitcast.4), custom_call_target="tpu_custom_call" | custom-call | tf_op jit(solution)/shard_map/pallas_call | solution.py:294
  65.2 2.1 %copy.8 = bf16[256,1536]{1,0:T(8,128)(2,1)} copy(bf16[256,1536]{1,0:T(8,128)(2,1)} %shard_map.64) | data formatting | bytes 1572864

commit v2 on v1

--- a/solution.py
+++ b/solution.py
@@ -20,12 +20,13 @@
 MESH = pl.DeviceIdType.MESH
 NEG = -1e30
 COLS = 256
+PLANE = 32
 
 
 def kernel(groups, tl_ref, cnt_ref, q_ref, k_ref, v_ref, w_ref, out_ref,
            kb0, kb1, kb2, vb0, vb1, vb2, qb0, qb1, qb2, ab0, ab1, ab2, ob0, ob1, ob2,
            wb0, wb1, wb2, to_right, to_left, acc, done,
-           ssem, rsem, hssem, hrsem, lsem, wsem, osem):
+           ssem, rsem, hssem, hrsem, lsem, wsem, osem, ack):
     t = lax.axis_index("temporal")
     u = lax.axis_index("ulysses")
     right, left, far = lax.rem(u + 1, RING), lax.rem(u + 3, RING), lax.rem(u + 2, RING)
@@ -192,22 +193,41 @@
 
         lax.fori_loop(0, acc.shape[1] // COLS, block, 0)
 
+    plane = min(PLANE, groups)
+    spot = lax.rem(t, plane)
+    head_of = lax.div(plane - 1 - spot, plane - 1)
+    second = lax.div(plane - 1 - lax.rem(spot + plane - 1, plane), plane - 1)
+    tail_of = lax.div(spot, plane - 1)
+    up, down = 1 - head_of - tail_of, head_of + second
     barrier = pltpu.get_barrier_semaphore()
-    for device in ((t, right), (t, left), (after, u), (before, u)):
-        pl.semaphore_signal(barrier, inc=1, device_id=device, device_id_type=MESH)
+
+    def tell(sem, device):
+        pl.semaphore_signal(sem, inc=1, device_id=device, device_id_type=MESH)
+
+    tell(barrier, (t, right))
+    tell(barrier, (t, left))
+    for flag, there in ((up, after), (down, before)):
+        pl.when(flag == 1)(functools.partial(tell, barrier, (there, u)))
     for s in range(9):
         local_copy(s).start()
+    pl.semaphore_wait(barrier, 4 - up - down)
+
+    start(0)
+    start(1)
+    for flag, there in ((up, after), (down, before)):
+        pl.when(flag == 0)(functools.partial(tell, ack, (there, u)))
     for head in range(LOCAL_HEADS):
         weight_copy(head).start()
-    pl.semaphore_wait(barrier, 4)
-
-    start(0)
-    start(1)
     relay(0)
     start(2)
     relay(1)
     start(3)
     collect(0)
+
+    @pl.when(up + down > 0)
+    def _():
+        pl.semaphore_wait(ack, up + down)
+
     halo_start(0, 0)
     relay(2)
     start(4)
@@ -313,6 +333,7 @@
                     pltpu.SemaphoreType.DMA((9,)),
                     pltpu.SemaphoreType.DMA((3,)),
                     pltpu.SemaphoreType.DMA,
+                    pltpu.SemaphoreType.REGULAR,
                 ]
             ),
             compiler_params=pltpu.CompilerParams(

time: 68.2 us -> 66.9 us (0.981)
  no operation moved by 1% of the time
where the time goes in v2:
time: 66.9 us; the launch traced here: 66.6 us
  Pallas kernels  64.5 us (96%)
  local copies, waits for them, and re-layouts  2.06 us (3%)
    pallas_call x1, Pallas kernels, on_device(): pl.pallas_call(functools.partial(kernel, groups), out_shape=jax.ShapeDtyp...  64.5 us
    unnamed x1, local copies, waits for them, and re-layouts  2.06 us

profile of v2, /device:TPU:6, one launch (start us, length us, event | category | flops | bytes accessed | tf_op | source)
XLA Modules:
  0.0 66.6 jit_solution(7372586231679702179)
XLA Ops:
  0.0 64.5 %shard_map.64 = bf16[256,1536]{1,0:T(8,128)(2,1)} custom-call(s32[8,5]{1,0:T(8,128)} %tl_ref.1, s32[8]{0:T(128)} %cnt_ref.1, bf16[2,128,1536]{2,1,0:T(8,128)(2,1)} %bitcast.5, bf16[2,128,1536]{2,1,0:T(8,128)(2,1)} %bitcast.6, bf16[2,128,1536]{2,1,0:T(8,128)(2,1)} %bitcast.7, bf16[4,3,128,1536]{3,2,1,0:T(8,128)(2,1)} %bitcast.4), custom_call_target="tpu_custom_call" | custom-call | tf_op jit(solution)/shard_map/pallas_call | solution.py:314
  64.5 2.1 %copy.8 = bf16[256,1536]{1,0:T(8,128)(2,1)} copy(bf16[256,1536]{1,0:T(8,128)(2,1)} %shard_map.64) | data formatting | bytes 1572864

commit v3 on v2

v3 whole, which is shorter than its diff:
```python
import functools
import math

import jax
import jax.numpy as jnp
from jax import lax
from jax.experimental import pallas as pl
from jax.experimental.pallas import tpu as pltpu
from jax.sharding import PartitionSpec as P

HD = 128
TILE = 128
REACH = 3
RING = 4
PAIR = 2
LOCAL_HEADS = 3
OWN = RING * PAIR
SPAN = OWN + 2 * REACH
SLOTS = 5
MESH = pl.DeviceIdType.MESH
NEG = -1e30
COLS = 256
BLOCKS = 6
PLANE = 32
ORDER = ((0, 0), (0, 1), (1, 0), (1, 1), (2, 0), (2, 1), (0, 2), (1, 2), (2, 2))


def kernel(groups, tl_ref, cnt_ref, q_ref, k_ref, v_ref, w_ref, out_ref,
           kb0, kb1, kb2, vb0, vb1, vb2, qb0, qb1, qb2, ab0, ab1, ab2, ob0, ob1, ob2,
           wb0, wb1, wb2, acc, done,
           ssem, rsem, hssem, hrsem, lsem, wsem, osem, ack):
    t = lax.axis_index("temporal")
    u = lax.axis_index("ulysses")
    right, left, far = lax.rem(u + 1, RING), lax.rem(u + 3, RING), lax.rem(u + 2, RING)
    after, before = lax.rem(t + 1, groups), lax.rem(t + groups - 1, groups)
    bufs = ((kb0, kb1, kb2), (vb0, vb1, vb2), (qb0, qb1, qb2))
    sources = (k_ref, v_ref, q_ref)
    joined, sent, weights = (ab0, ab1, ab2), (ob0, ob1, ob2), (wb0, wb1, wb2)

    def remote(src, dst, kind, index, device):
        return functools.partial(
            pltpu.make_async_remote_copy,
            src_ref=src, dst_ref=dst, send_sem=ssem.at[index, kind], recv_sem=rsem.at[index, kind],
            device_id=device, device_id_type=MESH)

    def columns(x, head):
        return pl.ds(pl.multiple_of((x * LOCAL_HEADS + head) * HD, HD), HD)

    def place(x):
        return pl.ds(pl.multiple_of(x * HD, HD), HD)

    def stage(s):
        head, kind = ORDER[s]
        base = REACH if kind < 2 else 0
        return sources[kind], bufs[kind][head], base, head

    def local_copy(s):
        src, buf, base, head = stage(s)
        return pltpu.make_async_copy(
            src.at[:, :, columns(u, head)], buf.at[pl.ds(base + PAIR * u, PAIR)], lsem.at[s])

    def weight_copy(head):
        return pltpu.make_async_copy(w_ref.at[:, head], weights[head], wsem.at[head])

    def sends(s, x):
        src, buf, base, head = stage(s)
        return (
            remote(src.at[0, :, columns(far, head)], buf.at[base + PAIR * x[0]], 0, s, (t, far)),
            remote(src.at[1, :, columns(far, head)], buf.at[base + PAIR * x[0] + 1], 1, s, (t, far)),
            remote(src.at[:, :, columns(right, head)], buf.at[pl.ds(base + PAIR * x[1], PAIR)], 2, s, (t, right)),
            remote(src.at[:, :, columns(left, head)], buf.at[pl.ds(base + PAIR * x[2], PAIR)], 3, s, (t, left)),
        )

    def collect(s):
        for copy in sends(s, (far, left, right)):
            copy().wait_recv()
        local_copy(s).wait()

    def halo(head, kind):
        buf = bufs[kind][head]
        return tuple(
            functools.partial(
                pltpu.make_async_remote_copy,
                src_ref=buf.at[pl.ds(low, REACH)], dst_ref=buf.at[pl.ds(high, REACH)],
                send_sem=hssem.at[head, kind, side], recv_sem=hrsem.at[head, kind, side],
                device_id=(there, u), device_id_type=MESH)
            for side, (low, high, there) in enumerate(((OWN, 0, after), (REACH, REACH + OWN, before))))

    def halo_wait(head):
        for kind in range(2):
            for copy in halo(head, kind):
                copy().wait_recv()

    def out_sends(head, x):
        s = 9 + head
        buf, dst = sent[head], joined[head]
        return (
            remote(buf.at[1, 0], dst.at[0, :, place(x[0])], 0, s, (t, far)),
            remote(buf.at[1, 1], dst.at[1, :, place(x[0])], 1, s, (t, far)),
            remote(buf.at[0], dst.at[:, :, place(x[1])], 2, s, (t, right)),
            remote(buf.at[2], dst.at[:, :, place(x[2])], 3, s, (t, left)),
        )

    def out_start(head, parts):
        copies = out_sends(head, (u, u, u))
        for part in parts:
            copies[part]().start()

    def out_collect(head):
        for copy in out_sends(head, (far, left, right)):
            copy().wait_recv()

    first_tile = t * OWN - REACH
    rate = math.log2(math.e) / math.sqrt(HD)

    def attend(head, offset):
        kb, vb, qb = bufs[0][head], bufs[1][head], bufs[2][head]
        base = PAIR * lax.rem(u + offset, RING)
        row = lax.broadcasted_iota(jnp.int32, (1, SLOTS * TILE), 1)
        for i in range(PAIR):
            g = base + i
            ids = [jnp.clip(tl_ref[g, slot] - first_tile, 0, SPAN - 1) for slot in range(SLOTS)]
            key_rows = jnp.concatenate([kb[n] for n in ids], axis=0)
            scores = lax.dot_general(qb[g], key_rows, (((1,), (1,)), ((), ())),
                                     preferred_element_type=jnp.float32)
            scores = jnp.where(row < cnt_ref[g] * TILE, scores, NEG)
            top = jnp.max(scores, axis=-1, keepdims=True)
            parts = jnp.exp2((scores - top) * rate)
            totals = jnp.sum(parts, axis=-1, keepdims=True)
            value_rows = jnp.concatenate([vb[n] for n in ids], axis=0)
            mixed = jnp.dot(parts.astype(jnp.bfloat16), value_rows, preferred_element_type=jnp.float32)
            mixed = (mixed / totals).astype(jnp.bfloat16)
            if offset == 0:
                joined[head][i, :, place(u)] = mixed
            else:
                sent[head][offset - 1, i] = mixed

    def project(head):
        rows = joined[head][...].reshape(PAIR * TILE, RING * HD)

        def product(c):
            cols = pl.ds(pl.multiple_of(c * COLS, COLS), COLS)
            w = weights[head][:, :, cols].reshape(RING * HD, COLS)
            return cols, jnp.dot(rows, w, preferred_element_type=jnp.float32)

        def block(c, carry):
            cols, part = product(c)
            acc[:, cols] = part + acc[:, cols] if head > 0 else part
            return carry

        if head < LOCAL_HEADS - 1:
            lax.fori_loop(0, BLOCKS, block, 0)
            return
        for c in range(BLOCKS):
            cols, part = product(c)
            done[:, cols] = (part + acc[:, cols]).astype(jnp.bfloat16)
            result(c).start()

    def result(c):
        cols = pl.ds(c * COLS, COLS)
        return pltpu.make_async_copy(done.at[:, cols], out_ref.at[:, cols], osem.at[c])

    plane = min(PLANE, groups)
    spot = lax.rem(t, plane)
    head_of = lax.div(plane - 1 - spot, plane - 1)
    second = lax.div(plane - 1 - lax.rem(spot + plane - 1, plane), plane - 1)
    tail_of = lax.div(spot, plane - 1)
    up, down = 1 - head_of - tail_of, head_of + second
    barrier = pltpu.get_barrier_semaphore()

    def tell(sem, device):
        pl.semaphore_signal(sem, inc=1, device_id=device, device_id_type=MESH)

    tell(barrier, (t, right))
    tell(barrier, (t, left))
    tell(barrier, (t, far))
    for flag, there in ((up, after), (down, before)):
        pl.when(flag == 1)(functools.partial(tell, barrier, (there, u)))
    for s in range(9):
        local_copy(s).start()
    pl.semaphore_wait(barrier, 5 - up - down)

    for s in range(9):
        for copy in sends(s, (u, u, u)):
            copy().start()
    for flag, there in ((up, after), (down, before)):
        pl.when(flag == 0)(functools.partial(tell, ack, (there, u)))
    for head in range(LOCAL_HEADS):
        weight_copy(head).start()
    for s in range(9):
        head, kind = ORDER[s]
        collect(s)
        if s == 0:
            @pl.when(up + down > 0)
            def _():
                pl.semaphore_wait(ack, up + down)
        if kind < 2:
            for copy in halo(head, kind):
                copy().start()
            continue
        halo_wait(head)
        attend(head, 2)
        out_start(head, (0, 1))
        attend(head, 1)
        out_start(head, (2,))
        attend(head, 3)
        out_start(head, (3,))
        attend(head, 0)
    for head in range(LOCAL_HEADS):
        weight_copy(head).wait()
        out_collect(head)
        project(head)

    for s in range(9):
        for copy in sends(s, (u, u, u)):
            copy().wait_send()
    for head in range(LOCAL_HEADS):
        for copy in out_sends(head, (u, u, u)):
            copy().wait_send()
        for kind in range(2):
            for copy in halo(head, kind):
                copy().wait_send()
    for c in range(BLOCKS):
        result(c).wait()


def solution(mesh):
    groups = mesh.shape["temporal"]

    def on_device(queries, keys, values, tile_list, counts, out_weight):
        width = queries.shape[1]
        split = lambda a: a.reshape(PAIR, TILE, width)
        any_space = pl.BlockSpec(memory_space=pl.ANY)
        smem = pl.BlockSpec(memory_space=pltpu.SMEM)
        bf = jnp.bfloat16
        heads = range(LOCAL_HEADS)
        return pl.pallas_call(
            functools.partial(kernel, groups),
            out_shape=jax.ShapeDtypeStruct(queries.shape, bf),
            in_specs=[smem, smem, any_space, any_space, any_space, any_space],
            out_specs=any_space,
            scratch_shapes=(
                [pltpu.VMEM((SPAN, TILE, HD), bf) for _ in range(2) for _ in heads]
                + [pltpu.VMEM((OWN, TILE, HD), bf) for _ in heads]
                + [pltpu.VMEM((PAIR, TILE, RING * HD), bf) for _ in heads]
                + [pltpu.VMEM((RING - 1, PAIR, TILE, HD), bf) for _ in heads]
                + [pltpu.VMEM((RING, HD, width), bf) for _ in heads]
                + [
                    pltpu.VMEM((PAIR * TILE, width), jnp.float32),
                    pltpu.VMEM((PAIR * TILE, width), bf),
                    pltpu.SemaphoreType.DMA((12, 4)),
                    pltpu.SemaphoreType.DMA((12, 4)),
                    pltpu.SemaphoreType.DMA((3, 2, 2)),
                    pltpu.SemaphoreType.DMA((3, 2, 2)),
                    pltpu.SemaphoreType.DMA((9,)),
                    pltpu.SemaphoreType.DMA((3,)),
                    pltpu.SemaphoreType.DMA((BLOCKS,)),
                    pltpu.SemaphoreType.REGULAR,
                ]
            ),
            compiler_params=pltpu.CompilerParams(
                collective_id=0, has_side_effects=True, vmem_limit_bytes=56 * 1024 * 1024
            ),
        )(tile_list, counts, split(queries), split(keys), split(values),
          out_weight.reshape(RING, LOCAL_HEADS, HD, width))

    rows = P(("temporal", "ulysses"), None)
    return jax.shard_map(
        on_device,
        mesh=mesh,
        in_specs=(rows, rows, rows, P("temporal", None), P("temporal"), P()),
        out_specs=rows,
        check_vma=False,
    )
```

time: 66.9 us -> 54.7 us (0.82)
  Pallas kernels: 64.5 us -> 52.5 us
    pallas_call x1, Pallas kernels: 64.5 us -> 52.5 us  [on_device(): pl.pallas_call(functools.partial(kernel, groups), out_shape=jax.ShapeDtyp...]
where the time goes in v3:
time: 54.7 us; the launch traced here: 54.5 us
  Pallas kernels  52.5 us (96%)
  local copies, waits for them, and re-layouts  2.06 us (4%)
    pallas_call x1, Pallas kernels, on_device(): pl.pallas_call(functools.partial(kernel, groups), out_shape=jax.ShapeDtyp...  52.5 us
    unnamed x1, local copies, waits for them, and re-layouts  2.06 us

profile of v3, /device:TPU:6, one launch (start us, length us, event | category | flops | bytes accessed | tf_op | source)
XLA Modules:
  0.0 54.5 jit_solution(7347634764292999602)
XLA Ops:
  0.0 52.5 %shard_map.64 = bf16[256,1536]{1,0:T(8,128)(2,1)} custom-call(s32[8,5]{1,0:T(8,128)} %tl_ref.1, s32[8]{0:T(128)} %cnt_ref.1, bf16[2,128,1536]{2,1,0:T(8,128)(2,1)} %bitcast.5, bf16[2,128,1536]{2,1,0:T(8,128)(2,1)} %bitcast.6, bf16[2,128,1536]{2,1,0:T(8,128)(2,1)} %bitcast.7, bf16[4,3,128,1536]{3,2,1,0:T(8,128)(2,1)} %bitcast.4), custom_call_target="tpu_custom_call" | custom-call | tf_op jit(solution)/shard_map/pallas_call | solution.py:237
  52.5 2.1 %copy.8 = bf16[256,1536]{1,0:T(8,128)(2,1)} copy(bf16[256,1536]{1,0:T(8,128)(2,1)} %shard_map.64) | data formatting | bytes 1572864
